TPU v7x, 32 devices: a whole 2x2x4 slice. The times are simulated.
32 devices in a mesh: row: 4 (over y, core), col: 8 (over z, x).
Axes of the slice: x: 2, y: 2, z: 4, core: 2. Of those that a mesh axis runs over, the one named last changes fastest.
Arguments:
- kernel: float32 [4, 4, 256, 2, 8, 256], P(None, 'row', None, None, 'col'), may hold values from -40 to 40, as said below
Outputs:
- trailing: float32 [4, 4, 256, 2, 8, 256], P(None, 'row', None, None, 'col')
- panels: float32 [4, 4, 256, 3, 256], P(None, 'row')
Inputs may be any that keep to these rules, and one draw needn't show every extreme that they name: kernel is symmetric and positive definite with smallest eigenvalue at least 1.
All inputs are finite; a program needn't handle non-finite values.
Results may differ from a plain program's by a relative error of at most 0.0003.
Values sent between devices are 32-bit elements; how exact they have to be, the bound alone decides.
A program may use at most 128 MiB of HBM per device.

v0:
```python
import jax
import jax.numpy as jnp
from jax import lax
from jax.sharding import PartitionSpec as P

STEPS = 3


def broadcast(value, axis, source):
    kept = jnp.where(lax.axis_index(axis) == source, value, 0).astype(value.dtype)
    return lax.psum(kept, axis)


def shards(kernel):
    row_tiles, _, tile_size, col_tiles, _, _ = kernel.shape
    row_count = lax.axis_size("row")
    col_count = lax.axis_size("col")
    row_index = lax.axis_index("row")
    col_index = lax.axis_index("col")
    stride = col_count // row_count
    working = kernel.reshape(row_tiles, tile_size, col_tiles, tile_size)
    identity = jnp.eye(tile_size, dtype=jnp.float32)
    tile_rows = jnp.arange(row_tiles) * row_count + row_index
    tile_cols = jnp.arange(col_tiles) * col_count + col_index
    collected = []
    for panel_step in range(STEPS):
        local_row = panel_step // row_count
        local_col = panel_step // col_count
        column_slab = working[:, :, local_col, :]
        diagonal = broadcast(column_slab[local_row], "row", panel_step % row_count)
        factor = jnp.linalg.cholesky(diagonal)
        inverse = lax.linalg.triangular_solve(factor, identity, left_side=True, lower=True)
        panel = jnp.einsum("art,st->ars", column_slab, inverse, precision=lax.Precision.HIGHEST)
        panel = jnp.where((tile_rows >= panel_step)[:, None, None], panel, jnp.float32(0.0))
        my_panel = broadcast(panel, "col", panel_step % col_count)
        collected.append(my_panel)
        selected = lax.dynamic_index_in_dim(
            my_panel.reshape(col_tiles, stride, tile_size, tile_size),
            col_index // row_count,
            1,
            keepdims=False,
        )
        gathered = lax.all_gather(selected, "row", axis=0, tiled=True)
        col_panel = lax.dynamic_index_in_dim(
            gathered.reshape(row_count, col_tiles, tile_size, tile_size),
            col_index % row_count,
            0,
            keepdims=False,
        )
        row_terms = jnp.where((tile_rows > panel_step)[:, None, None], my_panel, jnp.float32(0.0))
        col_terms = jnp.where((tile_cols > panel_step)[:, None, None], col_panel, jnp.float32(0.0))
        correction = jnp.einsum(
            "art,cst->arcs", row_terms, col_terms, precision=lax.Precision.HIGHEST
        )
        keep_mask = (tile_rows > panel_step)[:, None, None, None] & (tile_cols > panel_step)[
            None, None, :, None
        ]
        working = jnp.where(keep_mask, working - correction, jnp.float32(0.0))
    trailing = working.reshape(kernel.shape)
    panels = jnp.stack(collected, axis=2).reshape(row_tiles, 1, tile_size, STEPS, tile_size)
    return (trailing, panels)


def solution(mesh):
    in_specs = (P(None, "row", None, None, "col", None),)
    out_specs = (P(None, "row", None, None, "col", None), P(None, "row", None, None, None))
    return jax.shard_map(shards, mesh=mesh, in_specs=in_specs, out_specs=out_specs, check_vma=False)
```

profile of v0, /device:TPU:0, one launch (start us, length us, event | category | flops | bytes accessed | tf_op | source)
XLA Modules:
  0.0 669.3 jit_solution(3093933253821480764)
XLA Ops:
  7.2 4.6 copy.23
  11.8 0.7 fusion.24
  12.7 35.0 %all-reduce.8.cloned.1.call-done = f32[256,256]{0,1:T(8,128)} async-done(((f32[256,256]{0,1:T(8,128)}), f32[256,256]{0,1:T(8,128)}) %all-reduce.8.cloned.1.call-update) | async-done | bytes 262160 | tf_op jit(solution)/shard_map/psum | solution.py:11
  47.7 1.1 copy.24
  48.8 1.0 fusion.33
  49.8 11.7 %cholesky.172 = f32[128,128]{1,0:T(8,128)S(1)} custom-call(f32[128,128]{1,0:T(8,128)S(1)} %cholesky.270), custom_call_target="Cholesky" | custom-call | tf_op jit(solution)/shard_map/jit(cholesky)/cholesky | solution.py:31
  61.5 9.8 %custom-call.15 = f32[1,128,128]{1,2,0:T(8,128)S(1)} custom-call(f32[1,128,128]{2,1,0:T(8,128)S(1)} %get-tuple-element.72), custom_call_target="InvertDiagBlocksLowerTriangular" | custom-call | tf_op jit(solution)/shard_map/jit(cholesky)/cholesky | solution.py:31
  71.9 11.7 %cholesky.189 = f32[128,128]{1,0:T(8,128)S(1)} custom-call(f32[128,128]{1,0:T(8,128)S(1)} %convolution_subtract_fusion.5), custom_call_target="Cholesky" | custom-call | tf_op jit(solution)/shard_map/jit(cholesky)/cholesky | solution.py:31
  83.6 0.7 compare_reduce_fusion.4
  85.8 4.6 while.6
  86.9 1.4 bitcast_dynamic-update-slice_fusion.6
  89.0 1.4 bitcast_dynamic-update-slice_fusion.6
  90.4 19.7 %custom-call.16 = f32[2,128,128]{1,2,0:T(8,128)S(1)} custom-call(f32[2,128,128]{2,1,0:T(8,128)S(1)} %get-tuple-element.24), custom_call_target="InvertDiagBlocksLowerTriangular" | custom-call | tf_op jit(solution)/shard_map/triangular_solve/custom-call.0 | solution.py:32
  111.0 2.0 fusion.3
  113.1 78.4 %all-reduce.10.cloned.1.call-done = f32[4,256,256]{1,2,0:T(8,128)} async-done(((f32[4,256,256]{1,2,0:T(8,128)}), f32[4,256,256]{1,2,0:T(8,128)}) %all-reduce.10.cloned.1.call-update) | async-done | bytes 1048592 | tf_op jit(solution)/shard_map/psum | solution.py:11
  191.6 2.0 constant_dynamic-slice_fusion.5
  193.6 2.0 copy.60
  195.8 22.1 %all-gather.7.cloned.1.call-done = f32[8,1,256,256]{3,2,1,0:T(8,128)} async-done(((f32[2,1,256,256]{3,2,1,0:T(8,128)}), f32[8,1,256,256]{3,2,1,0:T(8,128)}) %all-gather.7.cloned.1.call-update) | async-done | bytes 2097168 | tf_op jit(solution)/shard_map/all_gather | solution.py:43
  217.9 3.2 subtract_select_fusion.1
  221.1 1.3 copy-done
  223.4 32.2 %all-reduce.12.cloned.1.call-done = f32[256,256]{0,1:T(8,128)} async-done(((f32[256,256]{0,1:T(8,128)}), f32[256,256]{0,1:T(8,128)}) %all-reduce.12.cloned.1.call-update) | async-done | bytes 262160 | tf_op jit(solution)/shard_map/psum | solution.py:11
  255.6 1.1 copy.29
  256.7 1.0 fusion.32
  258.4 11.7 %cholesky.206 = f32[128,128]{1,0:T(8,128)S(1)} custom-call(f32[128,128]{1,0:T(8,128)S(1)} %cholesky.273), custom_call_target="Cholesky" | custom-call | tf_op jit(solution)/shard_map/jit(cholesky)/cholesky | solution.py:31
  270.8 10.4 %custom-call.17 = f32[1,128,128]{1,2,0:T(8,128)} custom-call(f32[1,128,128]{2,1,0:T(8,128)S(1)} %get-tuple-element.68), custom_call_target="InvertDiagBlocksLowerTriangular" | custom-call | tf_op jit(solution)/shard_map/jit(cholesky)/cholesky | solution.py:31
  281.9 1.7 constant_dynamic-update-slice_fusion.1
  283.6 1.1 convolution_subtract_fusion.4
  284.7 11.7 %cholesky.223 = f32[128,128]{1,0:T(8,128)S(1)} custom-call(f32[128,128]{1,0:T(8,128)S(1)} %convolution_subtract_fusion.4), custom_call_target="Cholesky" | custom-call | tf_op jit(solution)/shard_map/jit(cholesky)/cholesky | solution.py:31
  299.1 0.7 select_select_fusion.1
  299.8 6.0 while.7
  300.7 2.2 bitcast_dynamic-update-slice_fusion.7
  303.7 2.2 bitcast_dynamic-update-slice_fusion.7
  306.5 20.5 %custom-call.18 = f32[2,128,128]{1,2,0:T(8,128)S(1)} custom-call(f32[2,128,128]{2,1,0:T(8,128)} %copy-done.7), custom_call_target="InvertDiagBlocksLowerTriangular" | custom-call | tf_op jit(solution)/shard_map/triangular_solve/custom-call.0 | solution.py:32
  327.3 1.1 convolution_subtract_fusion.1
  328.8 2.1 fusion.1
  330.9 78.4 %all-reduce.14.cloned.1.call-done = f32[4,256,256]{1,2,0:T(8,128)} async-done(((f32[4,256,256]{1,2,0:T(8,128)}), f32[4,256,256]{1,2,0:T(8,128)}) %all-reduce.14.cloned.1.call-update) | async-done | bytes 1048592 | tf_op jit(solution)/shard_map/psum | solution.py:11
  409.3 1.1 constant_dynamic-slice_fusion.4
  410.4 1.0 copy.61
  411.6 22.2 %all-gather.9.cloned.1.call-done = f32[8,1,256,256]{3,2,1,0:T(8,128)} async-done(((f32[2,1,256,256]{3,2,1,0:T(8,128)}), f32[8,1,256,256]{3,2,1,0:T(8,128)}) %all-gather.9.cloned.1.call-update) | async-done | bytes 2097168 | tf_op jit(solution)/shard_map/all_gather | solution.py:43
  433.8 4.2 subtract_select_fusion
  437.9 0.7 fusion.22
  439.0 32.1 %all-reduce.16.cloned.1.call-done = f32[256,256]{0,1:T(8,128)} async-done(((f32[256,256]{0,1:T(8,128)}), f32[256,256]{0,1:T(8,128)}) %all-reduce.16.cloned.1.call-update) | async-done | bytes 262160 | tf_op jit(solution)/shard_map/psum | solution.py:11
  471.1 1.8 copy.35
  472.9 1.1 fusion.31
  474.7 11.7 %cholesky.240 = f32[128,128]{1,0:T(8,128)S(1)} custom-call(f32[128,128]{1,0:T(8,128)S(1)} %cholesky.276), custom_call_target="Cholesky" | custom-call | tf_op jit(solution)/shard_map/jit(cholesky)/cholesky | solution.py:31
  487.1 10.4 %custom-call.19 = f32[1,128,128]{1,2,0:T(8,128)} custom-call(f32[1,128,128]{2,1,0:T(8,128)S(1)} %get-tuple-element.64), custom_call_target="InvertDiagBlocksLowerTriangular" | custom-call | tf_op jit(solution)/shard_map/jit(cholesky)/cholesky | solution.py:31
  498.2 1.7 constant_dynamic-update-slice_fusion
  499.9 1.1 convolution_subtract_fusion.3
  501.1 11.7 %cholesky.257 = f32[128,128]{1,0:T(8,128)S(1)} custom-call(f32[128,128]{1,0:T(8,128)S(1)} %convolution_subtract_fusion.3), custom_call_target="Cholesky" | custom-call | tf_op jit(solution)/shard_map/jit(cholesky)/cholesky | solution.py:31
  515.3 0.7 select_select_fusion
  516.1 6.0 while.8
  517.0 2.3 bitcast_dynamic-update-slice_fusion.8
  519.9 2.2 bitcast_dynamic-update-slice_fusion.8
  522.7 20.5 %custom-call.20 = f32[2,128,128]{1,2,0:T(8,128)S(1)} custom-call(f32[2,128,128]{2,1,0:T(8,128)} %copy-done.6), custom_call_target="InvertDiagBlocksLowerTriangular" | custom-call | tf_op jit(solution)/shard_map/triangular_solve/custom-call.0 | solution.py:32
  543.5 1.1 convolution_subtract_fusion
  545.0 2.1 fusion
  547.1 78.4 %all-reduce.18.cloned.1.call-done = f32[4,256,256]{1,2,0:T(8,128)} async-done(((f32[4,256,256]{1,2,0:T(8,128)}), f32[4,256,256]{1,2,0:T(8,128)}) %all-reduce.18.cloned.1.call-update) | async-done | bytes 1048592 | tf_op jit(solution)/shard_map/psum | solution.py:11
  625.5 1.9 constant_dynamic-slice_fusion.3
  627.4 2.0 copy.62
  629.5 3.4 maximum_bitcast_fusion
  632.9 3.6 copy.42
  636.6 15.2 %all-gather.11.cloned.1.call-done = f32[8,1,256,256]{3,2,1,0:T(8,128)} async-done(((f32[2,1,256,256]{3,2,1,0:T(8,128)}), f32[8,1,256,256]{3,2,1,0:T(8,128)}) %all-gather.11.cloned.1.call-update) | async-done | bytes 2097168 | tf_op jit(solution)/shard_map/all_gather | solution.py:43
  651.7 4.5 select_bitcast_fusion
  656.3 6.0 copy.41
  (90 shorter events, 16.6 us)
Async XLA Ops:
  7.2 40.5 %all-reduce.8.cloned.1.call-start = ((), (), s32[]{:S(2)}) async-start(), calls=%async_computation | async-start | bytes 524288 | tf_op jit(solution)/shard_map/psum | solution.py:11
  12.5 179.0 %all-reduce.10.cloned.1.call-start = ((), (), s32[]{:S(2)}) async-start(), calls=%async_computation.1 | async-start | bytes 2097152 | tf_op jit(solution)/shard_map/psum | solution.py:11
  113.1 104.9 %all-gather.7.cloned.1.call-start = ((), (), s32[]{:S(2)}) async-start(), calls=%async_computation.6 | async-start | bytes 2621440 | tf_op jit(solution)/shard_map/all_gather | solution.py:43
  191.6 26.3 %copy-start.2 = (f32[4,256,256]{1,2,0:T(8,128)S(1)}, f32[4,256,256]{1,2,0:T(8,128)}, u32[]{:S(2)}) copy-start(f32[4,256,256]{1,2,0:T(8,128)} %all-reduce.10.cloned.1.call-done) | copy-start | bytes 3145732
  195.6 60.0 %all-reduce.12.cloned.1.call-start = ((), (), s32[]{:S(2)}) async-start(), calls=%async_computation.2 | async-start | bytes 524288 | tf_op jit(solution)/shard_map/psum | solution.py:11
  221.1 1.3 copy-start
  223.2 186.2 %all-reduce.14.cloned.1.call-start = ((), (), s32[]{:S(2)}) async-start(), calls=%async_computation.3 | async-start | bytes 2097152 | tf_op jit(solution)/shard_map/psum | solution.py:11
  257.7 0.7 copy-start.4
  258.4 70.4 %copy-start.1 = (f32[4,256,2,256]{1,3,2,0:T(8,128)S(1)}, f32[4,256,2,256]{1,3,2,0:T(8,128)}, u32[]{:S(2)}) copy-start(f32[4,256,2,256]{1,3,2,0:T(8,128)} %copy-done) | copy-start | bytes 6291460
  305.9 0.6 copy-start.7
  330.8 102.9 %all-gather.9.cloned.1.call-start = ((), (), s32[]{:S(2)}) async-start(), calls=%async_computation.7 | async-start | bytes 2621440 | tf_op jit(solution)/shard_map/all_gather | solution.py:43
  411.4 59.7 %all-reduce.16.cloned.1.call-start = ((), (), s32[]{:S(2)}) async-start(), calls=%async_computation.4 | async-start | bytes 524288 | tf_op jit(solution)/shard_map/psum | solution.py:11
  438.7 186.8 %all-reduce.18.cloned.1.call-start = ((), (), s32[]{:S(2)}) async-start(), calls=%async_computation.5 | async-start | bytes 2097152 | tf_op jit(solution)/shard_map/psum | solution.py:11
  474.0 0.7 copy-start.5
  522.1 0.7 copy-start.6
  547.1 104.7 %all-gather.11.cloned.1.call-start = ((), (), s32[]{:S(2)}) async-start(), calls=%async_computation.8 | async-start | bytes 2621440 | tf_op jit(solution)/shard_map/all_gather | solution.py:43
  632.9 18.8 %copy-start.3 = (f32[4,256,256]{1,2,0:T(8,128)S(1)}, f32[4,256,256]{1,2,0:T(8,128)}, u32[]{:S(2)}) copy-start(f32[4,256,256]{1,2,0:T(8,128)} %all-reduce.18.cloned.1.call-done) | copy-start | bytes 3145732
Sparse Core Ops, SparseCore 0:
  12.7 34.9 all-reduce.7
  113.2 78.3 all-reduce.9
  195.7 22.1 all-gather.6
  223.3 32.2 all-reduce.11
  331.0 78.3 all-reduce.13
  411.6 22.1 all-gather.8
  438.8 32.2 all-reduce.15
  547.2 78.2 all-reduce.17
  629.5 22.1 all-gather.10
where the time goes:
time: 678 us; the launch traced here: 669 us
  waiting for transfers between devices  394 us (58%)
  other arithmetic  177 us (26%)
  local copies, waits for them, and re-layouts  49.2 us (7%)
  matrix products  28.4 us (4%)
  between operations  18.7 us (3%)
    psum x6, waiting for transfers between devices, broadcast(): return lax.psum(kept, axis)  335 us
    another operation x20, other arithmetic, shards(): factor = jnp.linalg.cholesky(diagonal)  106 us
    another operation x7, other arithmetic, shards(): lax.linalg.triangular_solve(factor, identity, left_side=True, lower=True)  62.2 us
    all_gather x3, waiting for transfers between devices, shards(): gathered = lax.all_gather(selected, 'row', axis=0, tiled=True)  59.5 us
    unnamed x22, local copies, waits for them, and re-layouts  23.3 us
    another operation x22, local copies, waits for them, and re-layouts, shards(): lax.linalg.triangular_solve(factor, identity, left_side=True, lower=True)  15.6 us
  transfers between devices with their start and end apart: 9, of which 9 were waited for; matrix products, arithmetic and copies ran while one was open for 1% of the time, Pallas kernels for 0%

commit v1 on v0

--- a/solution.py
+++ b/solution.py
@@ -4,6 +4,12 @@
 from jax.sharding import PartitionSpec as P
 
 STEPS = 3
+
+
+def launch_the_things(u_in, along_dim):
+    all_rows = list(u_in.shape[1:])
+    all_rows[along_dim] *= u_in.shape[0]
+    return jnp.moveaxis(u_in, 0, along_dim).reshape(all_rows)
 
 
 def broadcast(value, axis, source):
@@ -40,7 +46,22 @@
             1,
             keepdims=False,
         )
-        gathered = lax.all_gather(selected, "row", axis=0, tiled=True)
+
+        def lay_hubs(field_in, mesh_ax, dimension_no):
+            n_chips = lax.psum(1, mesh_ax)
+            rr = 0
+            row_list = []
+            while rr < n_chips:
+                row_list.append((rr, (rr + 1) % n_chips))
+                rr = rr + 1
+            cards = [field_in]
+            while len(cards) < n_chips:
+                cards.append(lax.ppermute(cards[-1], mesh_ax, row_list))
+            vec_out = lax.axis_index(mesh_ax)
+            cards = jnp.stack(cards, 0)[(vec_out - jnp.arange(n_chips)) % n_chips]
+            return launch_the_things(cards, dimension_no)
+
+        gathered = lay_hubs(selected, "row", 0)
         col_panel = lax.dynamic_index_in_dim(
             gathered.reshape(row_count, col_tiles, tile_size, tile_size),
             col_index % row_count,

time: 678 us -> 703 us (1.037)
  waiting for transfers between devices: 394 us -> 405 us
    ppermute x0 -> x9, waiting for transfers between devices: none -> 71 us  [lay_hubs(): cards.append(lax.ppermute(cards[-1], mesh_ax, row_list))]
    all_gather x3 -> x0, waiting for transfers between devices: 59.5 us -> none  [shards(): gathered = lax.all_gather(selected, 'row', axis=0, tiled=True)]
    gather x0 -> x3, local copies, waits for them, and re-layouts: none -> 9.36 us  [lay_hubs(): cards = jnp.stack(cards, 0)[(vec_out - jnp.arange(n_chips)) % n_chips]]
    unnamed x22 -> x33, local copies, waits for them, and re-layouts: 23.3 us -> 19.8 us
  transfers between devices with their start and end apart: 9 -> 15, of which waited for: 9 -> 15; matrix products, arithmetic and copies ran while one was open for 1% -> 1% of each run, Pallas kernels for 0% -> 0%
where the time goes in v1:
time: 703 us; the launch traced here: 693 us
  waiting for transfers between devices  405 us (58%)
  other arithmetic  184 us (26%)
  local copies, waits for them, and re-layouts  56.2 us (8%)
  matrix products  28.4 us (4%)
  between operations  18.7 us (3%)
    psum x6, waiting for transfers between devices, broadcast(): return lax.psum(kept, axis)  333 us
    another operation x20, other arithmetic, shards(): factor = jnp.linalg.cholesky(diagonal)  106 us
    ppermute x9, waiting for transfers between devices, lay_hubs(): cards.append(lax.ppermute(cards[-1], mesh_ax, row_list))  71 us
    another operation x7, other arithmetic, shards(): lax.linalg.triangular_solve(factor, identity, left_side=True, lower=True)  62.2 us
    unnamed x33, local copies, waits for them, and re-layouts  19.8 us
    another operation x22, local copies, waits for them, and re-layouts, shards(): lax.linalg.triangular_solve(factor, identity, left_side=True, lower=True)  15.1 us
  transfers between devices with their start and end apart: 15, of which 15 were waited for; matrix products, arithmetic and copies ran while one was open for 1% of the time, Pallas kernels for 0%

profile of v1, /device:TPU:0, one launch (start us, length us, event | category | flops | bytes accessed | tf_op | source)
XLA Modules:
  0.0 693.4 jit_solution(10936073787764377136)
XLA Ops:
  7.2 4.6 copy.20
  12.7 35.1 %all-reduce.8.cloned.1.call-done = f32[256,256]{0,1:T(8,128)} async-done(((f32[256,256]{0,1:T(8,128)}), f32[256,256]{0,1:T(8,128)}) %all-reduce.8.cloned.1.call-update) | async-done | bytes 262160 | tf_op jit(solution)/shard_map/psum | solution.py:17
  47.7 1.1 copy.21
  49.8 11.7 %cholesky.172 = f32[128,128]{1,0:T(8,128)S(1)} custom-call(f32[128,128]{1,0:T(8,128)S(1)} %cholesky.270), custom_call_target="Cholesky" | custom-call | tf_op jit(solution)/shard_map/jit(cholesky)/cholesky | solution.py:37
  61.5 9.8 %custom-call.15 = f32[1,128,128]{1,2,0:T(8,128)S(1)} custom-call(f32[1,128,128]{2,1,0:T(8,128)S(1)} %get-tuple-element.72), custom_call_target="InvertDiagBlocksLowerTriangular" | custom-call | tf_op jit(solution)/shard_map/jit(cholesky)/cholesky | solution.py:37
  71.9 11.7 %cholesky.189 = f32[128,128]{1,0:T(8,128)S(1)} custom-call(f32[128,128]{1,0:T(8,128)S(1)} %convolution_subtract_fusion.5), custom_call_target="Cholesky" | custom-call | tf_op jit(solution)/shard_map/jit(cholesky)/cholesky | solution.py:37
  85.7 4.1 while.6
  86.4 1.4 bitcast_dynamic-update-slice_fusion.6
  88.4 1.4 bitcast_dynamic-update-slice_fusion.6
  89.8 19.7 %custom-call.16 = f32[2,128,128]{1,2,0:T(8,128)S(1)} custom-call(f32[2,128,128]{2,1,0:T(8,128)S(1)} %get-tuple-element.24), custom_call_target="InvertDiagBlocksLowerTriangular" | custom-call | tf_op jit(solution)/shard_map/triangular_solve/custom-call.0 | solution.py:38
  110.4 2.0 fusion.3
  112.5 78.3 %all-reduce.10.cloned.1.call-done = f32[4,256,256]{1,2,0:T(8,128)} async-done(((f32[4,256,256]{1,2,0:T(8,128)}), f32[4,256,256]{1,2,0:T(8,128)}) %all-reduce.10.cloned.1.call-update) | async-done | bytes 1048592 | tf_op jit(solution)/shard_map/psum | solution.py:17
  192.2 8.6 %collective-permute-done = f32[2,256,256]{2,1,0:T(8,128)S(1)} collective-permute-done((f32[2,256,256]{2,1,0:T(8,128)S(1)}, f32[2,256,256]{2,1,0:T(8,128)S(1)}, u32[]{:S(2)}, u32[]{:S(2)}) %collective-permute-start) | collective-permute-done | bytes 524320 | tf_op jit(solution)/shard_map/ppermute | solution.py:59
  200.8 8.7 %collective-permute-done.1 = f32[2,256,256]{2,1,0:T(8,128)} collective-permute-done((f32[2,256,256]{2,1,0:T(8,128)S(1)}, f32[2,256,256]{2,1,0:T(8,128)}, u32[]{:S(2)}, u32[]{:S(2)}) %collective-permute-start.1) | collective-permute-done | bytes 524320 | tf_op jit(solution)/shard_map/ppermute | solution.py:59
  209.6 8.7 %collective-permute-done.2 = f32[2,256,256]{2,1,0:T(8,128)S(1)} collective-permute-done((f32[2,256,256]{2,1,0:T(8,128)}, f32[2,256,256]{2,1,0:T(8,128)S(1)}, u32[]{:S(2)}, u32[]{:S(2)}) %collective-permute-start.2) | collective-permute-done | bytes 524320 | tf_op jit(solution)/shard_map/ppermute | solution.py:59
  218.3 2.5 pad_maximum_fusion
  220.8 3.7 gather_fusion
  224.5 3.2 subtract_select_fusion.1
  227.7 1.3 copy-done
  230.0 31.8 %all-reduce.12.cloned.1.call-done = f32[256,256]{0,1:T(8,128)} async-done(((f32[256,256]{0,1:T(8,128)}), f32[256,256]{0,1:T(8,128)}) %all-reduce.12.cloned.1.call-update) | async-done | bytes 262160 | tf_op jit(solution)/shard_map/psum | solution.py:17
  261.8 1.1 copy.27
  264.6 11.7 %cholesky.206 = f32[128,128]{1,0:T(8,128)S(1)} custom-call(f32[128,128]{1,0:T(8,128)S(1)} %cholesky.273), custom_call_target="Cholesky" | custom-call | tf_op jit(solution)/shard_map/jit(cholesky)/cholesky | solution.py:37
  277.1 10.4 %custom-call.17 = f32[1,128,128]{1,2,0:T(8,128)} custom-call(f32[1,128,128]{2,1,0:T(8,128)S(1)} %get-tuple-element.68), custom_call_target="InvertDiagBlocksLowerTriangular" | custom-call | tf_op jit(solution)/shard_map/jit(cholesky)/cholesky | solution.py:37
  288.2 1.7 constant_dynamic-update-slice_fusion.1
  289.9 1.1 convolution_subtract_fusion.4
  291.0 11.7 %cholesky.223 = f32[128,128]{1,0:T(8,128)S(1)} custom-call(f32[128,128]{1,0:T(8,128)S(1)} %convolution_subtract_fusion.4), custom_call_target="Cholesky" | custom-call | tf_op jit(solution)/shard_map/jit(cholesky)/cholesky | solution.py:37
  306.1 5.8 while.7
  307.0 2.2 bitcast_dynamic-update-slice_fusion.7
  309.8 2.1 bitcast_dynamic-update-slice_fusion.7
  312.5 20.5 %custom-call.18 = f32[2,128,128]{1,2,0:T(8,128)S(1)} custom-call(f32[2,128,128]{2,1,0:T(8,128)} %copy-done.14), custom_call_target="InvertDiagBlocksLowerTriangular" | custom-call | tf_op jit(solution)/shard_map/triangular_solve/custom-call.0 | solution.py:38
  333.4 1.1 convolution_subtract_fusion.1
  334.8 2.1 fusion.1
  336.9 78.4 %all-reduce.14.cloned.1.call-done = f32[4,256,256]{1,2,0:T(8,128)} async-done(((f32[4,256,256]{1,2,0:T(8,128)}), f32[4,256,256]{1,2,0:T(8,128)}) %all-reduce.14.cloned.1.call-update) | async-done | bytes 1048592 | tf_op jit(solution)/shard_map/psum | solution.py:17
  416.6 8.6 %collective-permute-done.3 = f32[2,256,256]{2,1,0:T(8,128)S(1)} collective-permute-done((f32[2,256,256]{2,1,0:T(8,128)S(1)}, f32[2,256,256]{2,1,0:T(8,128)S(1)}, u32[]{:S(2)}, u32[]{:S(2)}) %collective-permute-start.3) | collective-permute-done | bytes 524320 | tf_op jit(solution)/shard_map/ppermute | solution.py:59
  425.2 8.6 %collective-permute-done.4 = f32[2,256,256]{2,1,0:T(8,128)S(1)} collective-permute-done((f32[2,256,256]{2,1,0:T(8,128)S(1)}, f32[2,256,256]{2,1,0:T(8,128)S(1)}, u32[]{:S(2)}, u32[]{:S(2)}) %collective-permute-start.4) | collective-permute-done | bytes 524320 | tf_op jit(solution)/shard_map/ppermute | solution.py:59
  433.9 8.5 %collective-permute-done.5 = f32[2,256,256]{2,1,0:T(8,128)S(1)} collective-permute-done((f32[2,256,256]{2,1,0:T(8,128)S(1)}, f32[2,256,256]{2,1,0:T(8,128)S(1)}, u32[]{:S(2)}, u32[]{:S(2)}) %collective-permute-start.5) | collective-permute-done | bytes 524320 | tf_op jit(solution)/shard_map/ppermute | solution.py:59
  443.2 1.7 pad_maximum_fusion.1
  445.0 2.0 gather_fusion.1
  447.0 4.2 subtract_select_fusion
  452.5 31.5 %all-reduce.16.cloned.1.call-done = f32[256,256]{0,1:T(8,128)} async-done(((f32[256,256]{0,1:T(8,128)}), f32[256,256]{0,1:T(8,128)}) %all-reduce.16.cloned.1.call-update) | async-done | bytes 262160 | tf_op jit(solution)/shard_map/psum | solution.py:17
  484.0 1.8 copy.34
  487.5 11.7 %cholesky.240 = f32[128,128]{1,0:T(8,128)S(1)} custom-call(f32[128,128]{1,0:T(8,128)S(1)} %cholesky.276), custom_call_target="Cholesky" | custom-call | tf_op jit(solution)/shard_map/jit(cholesky)/cholesky | solution.py:37
  500.0 10.4 %custom-call.19 = f32[1,128,128]{1,2,0:T(8,128)} custom-call(f32[1,128,128]{2,1,0:T(8,128)S(1)} %get-tuple-element.64), custom_call_target="InvertDiagBlocksLowerTriangular" | custom-call | tf_op jit(solution)/shard_map/jit(cholesky)/cholesky | solution.py:37
  511.1 1.7 constant_dynamic-update-slice_fusion
  512.9 1.1 convolution_subtract_fusion.3
  514.0 11.7 %cholesky.257 = f32[128,128]{1,0:T(8,128)S(1)} custom-call(f32[128,128]{1,0:T(8,128)S(1)} %convolution_subtract_fusion.3), custom_call_target="Cholesky" | custom-call | tf_op jit(solution)/shard_map/jit(cholesky)/cholesky | solution.py:37
  529.0 5.9 while.8
  529.8 2.3 bitcast_dynamic-update-slice_fusion.8
  532.7 2.2 bitcast_dynamic-update-slice_fusion.8
  535.6 20.5 %custom-call.20 = f32[2,128,128]{1,2,0:T(8,128)S(1)} custom-call(f32[2,128,128]{2,1,0:T(8,128)} %copy-done.13), custom_call_target="InvertDiagBlocksLowerTriangular" | custom-call | tf_op jit(solution)/shard_map/triangular_solve/custom-call.0 | solution.py:38
  556.4 1.1 convolution_subtract_fusion
  557.8 2.1 fusion
  559.9 78.4 %all-reduce.18.cloned.1.call-done = f32[4,256,256]{1,2,0:T(8,128)} async-done(((f32[4,256,256]{1,2,0:T(8,128)}), f32[4,256,256]{1,2,0:T(8,128)}) %all-reduce.18.cloned.1.call-update) | async-done | bytes 1048592 | tf_op jit(solution)/shard_map/psum | solution.py:17
  638.3 1.9 constant_dynamic-slice_fusion.3
  640.2 2.1 copy.37
  642.2 8.8 %collective-permute-done.6 = f32[2,256,256]{2,1,0:T(8,128)S(1)} collective-permute-done((f32[2,256,256]{2,1,0:T(8,128)}, f32[2,256,256]{2,1,0:T(8,128)S(1)}, u32[]{:S(2)}, u32[]{:S(2)}) %collective-permute-start.6) | collective-permute-done | bytes 524320 | tf_op jit(solution)/shard_map/ppermute | solution.py:59
  651.9 8.7 %collective-permute-done.7 = f32[2,256,256]{2,1,0:T(8,128)} collective-permute-done((f32[2,256,256]{2,1,0:T(8,128)S(1)}, f32[2,256,256]{2,1,0:T(8,128)}, u32[]{:S(2)}, u32[]{:S(2)}) %collective-permute-start.7) | collective-permute-done | bytes 524320 | tf_op jit(solution)/shard_map/ppermute | solution.py:59
  660.7 3.4 maximum_bitcast_fusion
  664.1 3.6 copy.42
  667.7 1.8 collective-permute-done.8
  669.5 2.7 pad_maximum_fusion.2
  672.2 3.7 gather_fusion.2
  675.9 4.5 select_bitcast_fusion
  680.3 6.0 copy.41
  (121 shorter events, 27.6 us)
Async XLA Ops:
  7.2 40.5 %all-reduce.8.cloned.1.call-start = ((), (), s32[]{:S(2)}) async-start(), calls=%async_computation | async-start | bytes 524288 | tf_op jit(solution)/shard_map/psum | solution.py:17
  12.5 178.3 %all-reduce.10.cloned.1.call-start = ((), (), s32[]{:S(2)}) async-start(), calls=%async_computation.1 | async-start | bytes 2097152 | tf_op jit(solution)/shard_map/psum | solution.py:17
  112.4 149.4 %all-reduce.12.cloned.1.call-start = ((), (), s32[]{:S(2)}) async-start(), calls=%async_computation.2 | async-start | bytes 524288 | tf_op jit(solution)/shard_map/psum | solution.py:17
  192.1 8.7 %collective-permute-start = (f32[2,256,256]{2,1,0:T(8,128)S(1)}, f32[2,256,256]{2,1,0:T(8,128)S(1)}, u32[]{:S(2)}, u32[]{:S(2)}) collective-permute-start(f32[2,256,256]{2,1,0:T(8,128)S(1)} %bitcast.195), channel_id=1, source_target_pairs={{0,8},{8,16},{16,24},{24,0},{1,9},{9,17},{17,25},{25,1},{2,10},{10... | collective-permute-start | bytes 1572872 | tf_op jit(solution)/shard_map/ppermute | solution.py:59
  200.8 8.7 %collective-permute-start.1 = (f32[2,256,256]{2,1,0:T(8,128)S(1)}, f32[2,256,256]{2,1,0:T(8,128)}, u32[]{:S(2)}, u32[]{:S(2)}) collective-permute-start(f32[2,256,256]{2,1,0:T(8,128)S(1)} %collective-permute-done), channel_id=1, source_target_pairs={{0,8},{8,16},{16,24},{24,0},{1,9},{9,17},{17,25},{25,1},{2,10},{10... | collective-permute-start | bytes 1572872 | tf_op jit(solution)/shard_map/ppermute | solution.py:59
  209.5 8.8 %collective-permute-start.2 = (f32[2,256,256]{2,1,0:T(8,128)}, f32[2,256,256]{2,1,0:T(8,128)S(1)}, u32[]{:S(2)}, u32[]{:S(2)}) collective-permute-start(f32[2,256,256]{2,1,0:T(8,128)} %collective-permute-done.1), channel_id=1, source_target_pairs={{0,8},{8,16},{16,24},{24,0},{1,9},{9,17},{17,25},{25,1},{2,10},{10... | collective-permute-start | bytes 1572872 | tf_op jit(solution)/shard_map/ppermute | solution.py:59
  220.8 3.7 copy-start.2
  227.7 1.3 copy-start
  229.8 185.5 %all-reduce.14.cloned.1.call-start = ((), (), s32[]{:S(2)}) async-start(), calls=%async_computation.3 | async-start | bytes 2097152 | tf_op jit(solution)/shard_map/psum | solution.py:17
  263.9 0.7 copy-start.6
  264.6 70.2 %copy-start.1 = (f32[4,256,2,256]{1,3,2,0:T(8,128)S(1)}, f32[4,256,2,256]{1,3,2,0:T(8,128)}, u32[]{:S(2)}) copy-start(f32[4,256,2,256]{1,3,2,0:T(8,128)} %copy-done) | copy-start | bytes 6291460
  311.9 0.7 copy-start.14
  336.9 147.1 %all-reduce.16.cloned.1.call-start = ((), (), s32[]{:S(2)}) async-start(), calls=%async_computation.4 | async-start | bytes 524288 | tf_op jit(solution)/shard_map/psum | solution.py:17
  416.6 25.9 %copy-start.5 = (f32[2,1,256,256]{3,2,0,1:T(8,128)}, f32[2,1,256,256]{3,2,0,1:T(8,128)S(1)}, u32[]{:S(2)}) copy-start(f32[2,1,256,256]{3,2,0,1:T(8,128)S(1)} %copy.30) | copy-start | bytes 1572868
  416.6 8.7 %collective-permute-start.3 = (f32[2,256,256]{2,1,0:T(8,128)S(1)}, f32[2,256,256]{2,1,0:T(8,128)S(1)}, u32[]{:S(2)}, u32[]{:S(2)}) collective-permute-start(f32[2,256,256]{2,1,0:T(8,128)S(1)} %bitcast.199), channel_id=1, source_target_pairs={{0,8},{8,16},{16,24},{24,0},{1,9},{9,17},{17,25},{25,1},{2,10},{10... | collective-permute-start | bytes 1572872 | tf_op jit(solution)/shard_map/ppermute | solution.py:59
  425.2 17.2 %copy-start.10 = (f32[2,256,256]{2,1,0:T(8,128)}, f32[2,256,256]{2,1,0:T(8,128)S(1)}, u32[]{:S(2)}) copy-start(f32[2,256,256]{2,1,0:T(8,128)S(1)} %collective-permute-done.3) | copy-start | bytes 1572868
  425.2 8.6 %collective-permute-start.4 = (f32[2,256,256]{2,1,0:T(8,128)S(1)}, f32[2,256,256]{2,1,0:T(8,128)S(1)}, u32[]{:S(2)}, u32[]{:S(2)}) collective-permute-start(f32[2,256,256]{2,1,0:T(8,128)S(1)} %collective-permute-done.3), channel_id=1, source_target_pairs={{0,8},{8,16},{16,24},{24,0},{1,9},{9,17},{17,25},{25,1},{2,10},{10... | collective-permute-start | bytes 1572872 | tf_op jit(solution)/shard_map/ppermute | solution.py:59
  433.8 8.6 %copy-start.11 = (f32[2,256,256]{2,1,0:T(8,128)}, f32[2,256,256]{2,1,0:T(8,128)S(1)}, u32[]{:S(2)}) copy-start(f32[2,256,256]{2,1,0:T(8,128)S(1)} %collective-permute-done.4) | copy-start | bytes 1572868
  433.8 8.6 %collective-permute-start.5 = (f32[2,256,256]{2,1,0:T(8,128)S(1)}, f32[2,256,256]{2,1,0:T(8,128)S(1)}, u32[]{:S(2)}, u32[]{:S(2)}) collective-permute-start(f32[2,256,256]{2,1,0:T(8,128)S(1)} %collective-permute-done.4), channel_id=1, source_target_pairs={{0,8},{8,16},{16,24},{24,0},{1,9},{9,17},{17,25},{25,1},{2,10},{10... | collective-permute-start | bytes 1572872 | tf_op jit(solution)/shard_map/ppermute | solution.py:59
  442.5 0.8 copy-start.12
  451.9 186.4 %all-reduce.18.cloned.1.call-start = ((), (), s32[]{:S(2)}) async-start(), calls=%async_computation.5 | async-start | bytes 2097152 | tf_op jit(solution)/shard_map/psum | solution.py:17
  486.8 0.7 copy-start.7
  534.9 0.7 copy-start.13
  642.2 8.8 %collective-permute-start.6 = (f32[2,256,256]{2,1,0:T(8,128)}, f32[2,256,256]{2,1,0:T(8,128)S(1)}, u32[]{:S(2)}, u32[]{:S(2)}) collective-permute-start(f32[2,256,256]{2,1,0:T(8,128)} %bitcast.197), channel_id=1, source_target_pairs={{0,8},{8,16},{16,24},{24,0},{1,9},{9,17},{17,25},{25,1},{2,10},{10... | collective-permute-start | bytes 1572872 | tf_op jit(solution)/shard_map/ppermute | solution.py:59
  651.1 0.8 copy-start.8
  651.9 8.7 %collective-permute-start.7 = (f32[2,256,256]{2,1,0:T(8,128)S(1)}, f32[2,256,256]{2,1,0:T(8,128)}, u32[]{:S(2)}, u32[]{:S(2)}) collective-permute-start(f32[2,256,256]{2,1,0:T(8,128)S(1)} %collective-permute-done.6), channel_id=1, source_target_pairs={{0,8},{8,16},{16,24},{24,0},{1,9},{9,17},{17,25},{25,1},{2,10},{10... | collective-permute-start | bytes 1572872 | tf_op jit(solution)/shard_map/ppermute | solution.py:59
  660.6 8.9 %collective-permute-start.8 = (f32[2,256,256]{2,1,0:T(8,128)}, f32[2,256,256]{2,1,0:T(8,128)}, u32[]{:S(2)}, u32[]{:S(2)}) collective-permute-start(f32[2,256,256]{2,1,0:T(8,128)} %collective-permute-done.7), channel_id=1, source_target_pairs={{0,8},{8,16},{16,24},{24,0},{1,9},{9,17},{17,25},{25,1},{2,10},{10... | collective-permute-start | bytes 1572872 | tf_op jit(solution)/shard_map/ppermute | solution.py:59
  664.1 5.4 copy-start.4
  664.1 5.4 copy-start.9
  672.2 3.7 copy-start.3
Sparse Core Ops, SparseCore 0:
  12.7 34.9 all-reduce.7
  112.5 78.2 all-reduce.9
  229.9 31.8 all-reduce.11
  337.0 78.2 all-reduce.13
  452.0 31.8 all-reduce.15
  560.0 78.2 all-reduce.17
